TPU v7x, 32 devices: a whole 2x2x4 slice. The times are simulated.
32 devices in a mesh: dp: 8 (over y, x, core), seq: 4 (over z).
Axes of the slice: x: 2, y: 2, z: 4, core: 2. Of those that a mesh axis runs over, the one named last changes fastest.
Arguments:
- tokens_in: bfloat16 [16, 580, 1024], P('dp', 'seq'), may hold values from -6 to 6
- cotangent: bfloat16 [16, 580, 1024], P('dp', 'seq'), may hold values from -6 to 6
- group_count: int32 [8], P('dp'), may hold values from 1 to 2, as said below
- key_mask: int32 [16, 580], P('dp'), may hold values from 0 to 1, as said below
- ln1_gain: float32 [1024], P(('dp', 'seq')), may hold values from 0.5 to 1.5
- ln1_shift: float32 [1024], P(('dp', 'seq')), may hold values from -3 to 3
- w_query: float32 [1024, 1024], P(('dp', 'seq')), may hold values from -0.25 to 0.25
- b_query: float32 [1024], P(('dp', 'seq')), may hold values from -3 to 3
- w_key: float32 [1024, 1024], P(('dp', 'seq')), may hold values from -0.1875 to 0.1875
- w_value: float32 [1024, 1024], P(('dp', 'seq')), may hold values from -0.1875 to 0.1875
- b_value: float32 [1024], P(('dp', 'seq')), may hold values from -0.6 to 0.6
- w_out: float32 [1024, 1024], P(('dp', 'seq')), may hold values from -1.5 to 1.5
- b_out: float32 [1024], P(('dp', 'seq')), may hold values from -3 to 3
- ln2_gain: float32 [1024], P(('dp', 'seq')), may hold values from 0.5 to 1.5
- ln2_shift: float32 [1024], P(('dp', 'seq')), may hold values from -3 to 3
- w_up: float32 [1024, 4096], P(('dp', 'seq')), may hold values from -0.1875 to 0.1875
- b_up: float32 [4096], P(('dp', 'seq')), may hold values from -3 to 3
- w_down: float32 [4096, 1024], P(('dp', 'seq')), may hold values from -0.09375 to 0.09375
- b_down: float32 [1024], P(('dp', 'seq')), may hold values from -3 to 3
Outputs:
- block_out: bfloat16 [16, 580, 1024], P('dp', 'seq')
- input_grad: bfloat16 [16, 580, 1024], P('dp', 'seq')
- grad_ln1_gain: float32 [1024], P(('dp', 'seq'))
- grad_ln1_shift: float32 [1024], P(('dp', 'seq'))
- grad_w_query: float32 [1024, 1024], P(('dp', 'seq'))
- grad_b_query: float32 [1024], P(('dp', 'seq'))
- grad_w_key: float32 [1024, 1024], P(('dp', 'seq'))
- grad_w_value: float32 [1024, 1024], P(('dp', 'seq'))
- grad_b_value: float32 [1024], P(('dp', 'seq'))
- grad_w_out: float32 [1024, 1024], P(('dp', 'seq'))
- grad_b_out: float32 [1024], P(('dp', 'seq'))
- grad_ln2_gain: float32 [1024], P(('dp', 'seq'))
- grad_ln2_shift: float32 [1024], P(('dp', 'seq'))
- grad_w_up: float32 [1024, 4096], P(('dp', 'seq'))
- grad_b_up: float32 [4096], P(('dp', 'seq'))
- grad_w_down: float32 [4096, 1024], P(('dp', 'seq'))
- grad_b_down: float32 [1024], P(('dp', 'seq'))
Inputs may be any that keep to these rules, and one draw needn't show every extreme that they name: A data group's images fill its first group_count slots; some group holds 2. `key_mask`: the first token of every image is a key; positions 577 and later never are.
All inputs are finite; a program needn't handle non-finite values.
Results may differ from a plain program's by a relative error of at most 0.013.
The roundings to bfloat16 on the way count: a program that leaves them out, or rounds other values in their place, can miss the bound.
Values may be sent and summed in bfloat16 or wider, within the bound.
No kernel may reach another device: no remote copies, remote signals or barrier semaphores. Data moves between devices by JAX's collectives and lax.ppermute only.
A program may use at most 192 MiB of HBM per device.

v0:
```python
import jax
import jax.numpy as jnp
from jax import lax
from jax.sharding import PartitionSpec as P

HD = 64
EPSILON = 1e-05
SLOPE = 1.702
MASKED = -1000000000.0


def norm_stats(values):
    center = values - jnp.mean(values, axis=-1, keepdims=True)
    inverse = lax.rsqrt(jnp.mean(center * center, axis=-1, keepdims=True) + EPSILON)
    return (center * inverse, inverse)


def norm_back(incoming, normal, inverse, gain):
    scaled = incoming * gain
    rows_grad = inverse * (
        scaled
        - jnp.mean(scaled, axis=-1, keepdims=True)
        - normal * jnp.mean(scaled * normal, axis=-1, keepdims=True)
    )
    return (rows_grad, jnp.sum(incoming * normal, axis=0), jnp.sum(incoming, axis=0))


def product(left, right):
    return jnp.dot(left, right, preferred_element_type=jnp.float32)


def contract_rows(left, right):
    return lax.dot_general(
        left, right, (((0,), (0,)), ((), ())), preferred_element_type=jnp.float32
    )


def contract_cols(left, right):
    return lax.dot_general(
        left, right, (((1,), (1,)), ((), ())), preferred_element_type=jnp.float32
    )


def split_heads(stacked):
    length = stacked.shape[0]
    heads_here = stacked.shape[2] // HD
    queries = stacked[:, 0].reshape(length, heads_here, HD)
    keys_all = stacked[:, 1].reshape(length, heads_here, HD)
    values_all = stacked[:, 2].reshape(length, heads_here, HD)
    return (queries, keys_all, values_all)


def masked_scores(queries, keys_all, key_keep):
    scores = jnp.einsum(
        "qhd,khd->hqk", queries, keys_all, preferred_element_type=jnp.float32
    ) * HD ** (-0.5)
    return jnp.where(key_keep[None, None, :] > 0, scores, MASKED)


def attend_image(paired):
    stacked, key_keep = paired
    queries, keys_all, values_all = split_heads(stacked)
    scores = masked_scores(queries, keys_all, key_keep)
    row_peak = jnp.max(scores, axis=-1, keepdims=True)
    weights_exp = jnp.exp(scores - row_peak)
    row_total = jnp.sum(weights_exp, axis=-1, keepdims=True)
    weights_soft = weights_exp / row_total
    mixed_out = jnp.einsum(
        "hqk,khd->qhd",
        weights_soft.astype(jnp.bfloat16),
        values_all,
        preferred_element_type=jnp.float32,
    )
    log_total = (row_peak + jnp.log(row_total))[..., 0]
    return (mixed_out.reshape(stacked.shape[0], stacked.shape[2]).astype(jnp.bfloat16), log_total)


def attend_back(packed):
    stacked, grad_mixed, log_total, key_keep = packed
    queries, keys_all, values_all = split_heads(stacked)
    scores = masked_scores(queries, keys_all, key_keep)
    weights_soft = jnp.exp(scores - log_total[..., None])
    grad_mix = grad_mixed.reshape(queries.shape)
    grad_values = jnp.einsum(
        "hqk,qhd->khd",
        weights_soft.astype(jnp.bfloat16),
        grad_mix,
        preferred_element_type=jnp.float32,
    )
    grad_weights = jnp.einsum(
        "qhd,khd->hqk", grad_mix, values_all, preferred_element_type=jnp.float32
    )
    row_inner = jnp.sum(grad_weights * weights_soft, axis=-1, keepdims=True)
    grad_scores = (weights_soft * (grad_weights - row_inner)).astype(jnp.bfloat16)
    grad_queries = jnp.einsum(
        "hqk,khd->qhd", grad_scores, keys_all, preferred_element_type=jnp.float32
    ) * HD ** (-0.5)
    grad_keys = jnp.einsum(
        "hqk,qhd->khd", grad_scores, queries, preferred_element_type=jnp.float32
    ) * HD ** (-0.5)
    length = stacked.shape[0]
    return jnp.stack(
        [
            grad_queries.reshape(length, -1),
            grad_keys.reshape(length, -1),
            grad_values.reshape(length, -1),
        ],
        axis=1,
    ).astype(jnp.bfloat16)


def per_device(
    tokens_in,
    cotangent,
    group_count,
    key_mask,
    ln1_gain,
    ln1_shift,
    w_query,
    b_query,
    w_key,
    w_value,
    b_value,
    w_out,
    b_out,
    ln2_gain,
    ln2_shift,
    w_up,
    b_up,
    w_down,
    b_down,
):
    slot_count, tok_dev, width = tokens_in.shape
    row_count = slot_count * tok_dev
    shared = (
        lax.all_gather(ln1_gain.astype(jnp.bfloat16), ("dp", "seq"), axis=0, tiled=True),
        lax.all_gather(ln1_shift.astype(jnp.bfloat16), ("dp", "seq"), axis=0, tiled=True),
        lax.all_gather(w_query.astype(jnp.bfloat16), ("dp", "seq"), axis=0, tiled=True),
        lax.all_gather(b_query.astype(jnp.bfloat16), ("dp", "seq"), axis=0, tiled=True),
        lax.all_gather(w_key.astype(jnp.bfloat16), ("dp", "seq"), axis=0, tiled=True),
        lax.all_gather(w_value.astype(jnp.bfloat16), ("dp", "seq"), axis=0, tiled=True),
        lax.all_gather(b_value.astype(jnp.bfloat16), ("dp", "seq"), axis=0, tiled=True),
        lax.all_gather(w_out.astype(jnp.bfloat16), ("dp", "seq"), axis=0, tiled=True),
        lax.all_gather(b_out.astype(jnp.bfloat16), ("dp", "seq"), axis=0, tiled=True),
        lax.all_gather(ln2_gain.astype(jnp.bfloat16), ("dp", "seq"), axis=0, tiled=True),
        lax.all_gather(ln2_shift.astype(jnp.bfloat16), ("dp", "seq"), axis=0, tiled=True),
        lax.all_gather(w_up.astype(jnp.bfloat16), ("dp", "seq"), axis=0, tiled=True),
        lax.all_gather(b_up.astype(jnp.bfloat16), ("dp", "seq"), axis=0, tiled=True),
        lax.all_gather(w_down.astype(jnp.bfloat16), ("dp", "seq"), axis=0, tiled=True),
        lax.all_gather(b_down.astype(jnp.bfloat16), ("dp", "seq"), axis=0, tiled=True),
    )
    (
        gain_one,
        shift_one,
        query_w,
        query_b,
        key_w,
        value_w,
        value_b,
        out_w,
        out_b,
        gain_two,
        shift_two,
        up_w,
        up_b,
        down_w,
        down_b,
    ) = shared
    live_slot = (jnp.arange(slot_count) < group_count[0]).astype(jnp.float32)[:, None, None]
    inputs = tokens_in.astype(jnp.float32).reshape(row_count, width)
    normal_one, inverse_one = norm_stats(inputs)
    normed_one = (normal_one * gain_one + shift_one).astype(jnp.bfloat16)
    queries = (product(normed_one, query_w) + query_b).astype(jnp.bfloat16)
    keys_all = product(normed_one, key_w).astype(jnp.bfloat16)
    values_all = (product(normed_one, value_w) + value_b).astype(jnp.bfloat16)
    stacked = jnp.stack([queries, keys_all, values_all], axis=1).reshape(
        slot_count, tok_dev, 3, width
    )
    by_heads = lax.all_to_all(stacked, "seq", split_axis=3, concat_axis=1, tiled=True)
    mixed_heads, log_total = lax.map(attend_image, (by_heads, key_mask))
    mixed_tok = lax.all_to_all(mixed_heads, "seq", split_axis=1, concat_axis=2, tiled=True).reshape(
        row_count, width
    )
    middle = inputs + product(mixed_tok, out_w) + out_b
    normal_two, inverse_two = norm_stats(middle)
    normed_two = (normal_two * gain_two + shift_two).astype(jnp.bfloat16)
    hidden = product(normed_two, up_w) + up_b
    gate_sig = jax.nn.sigmoid(SLOPE * hidden)
    activated = (hidden * gate_sig).astype(jnp.bfloat16)
    result = middle + product(activated, down_w) + down_b
    block_out = (result.reshape(slot_count, tok_dev, width) * live_slot).astype(jnp.bfloat16)
    upstream = (cotangent.astype(jnp.float32) * live_slot).reshape(row_count, width)
    upstream_low = upstream.astype(jnp.bfloat16)
    grad_down = contract_rows(activated, upstream_low)
    grad_down_b = jnp.sum(upstream, axis=0)
    grad_act = contract_cols(upstream_low, down_w)
    grad_hidden = (grad_act * (gate_sig + SLOPE * hidden * gate_sig * (1.0 - gate_sig))).astype(
        jnp.bfloat16
    )
    grad_up = contract_rows(normed_two, grad_hidden)
    grad_up_b = jnp.sum(grad_hidden.astype(jnp.float32), axis=0)
    grad_normed_two = contract_cols(grad_hidden, up_w)
    grad_mid, grad_gain_two, grad_shift_two = norm_back(
        grad_normed_two, normal_two, inverse_two, gain_two
    )
    grad_middle = upstream + grad_mid
    branch_low = grad_middle.astype(jnp.bfloat16)
    grad_out = contract_rows(mixed_tok, branch_low)
    grad_out_b = jnp.sum(branch_low.astype(jnp.float32), axis=0)
    grad_mixed = (
        contract_cols(branch_low, out_w).astype(jnp.bfloat16).reshape(slot_count, tok_dev, width)
    )
    grad_by_heads = lax.all_to_all(grad_mixed, "seq", split_axis=2, concat_axis=1, tiled=True)
    grad_stacked = lax.map(attend_back, (by_heads, grad_by_heads, log_total, key_mask))
    grad_tok = lax.all_to_all(grad_stacked, "seq", split_axis=1, concat_axis=3, tiled=True).reshape(
        row_count, 3, width
    )
    grad_q_rows = grad_tok[:, 0]
    grad_k_rows = grad_tok[:, 1]
    grad_v_rows = grad_tok[:, 2]
    grad_query = contract_rows(normed_one, grad_q_rows)
    grad_query_b = jnp.sum(grad_q_rows.astype(jnp.float32), axis=0)
    grad_key = contract_rows(normed_one, grad_k_rows)
    grad_value = contract_rows(normed_one, grad_v_rows)
    grad_value_b = jnp.sum(grad_v_rows.astype(jnp.float32), axis=0)
    grad_normed_one = (
        contract_cols(grad_q_rows, query_w)
        + contract_cols(grad_k_rows, key_w)
        + contract_cols(grad_v_rows, value_w)
    )
    grad_first, grad_gain_one, grad_shift_one = norm_back(
        grad_normed_one, normal_one, inverse_one, gain_one
    )
    input_grad = (grad_middle + grad_first).astype(jnp.bfloat16).reshape(slot_count, tok_dev, width)
    every_shard = (
        lax.psum_scatter(grad_gain_one, ("dp", "seq"), scatter_dimension=0, tiled=True),
        lax.psum_scatter(grad_shift_one, ("dp", "seq"), scatter_dimension=0, tiled=True),
        lax.psum_scatter(grad_query, ("dp", "seq"), scatter_dimension=0, tiled=True),
        lax.psum_scatter(grad_query_b, ("dp", "seq"), scatter_dimension=0, tiled=True),
        lax.psum_scatter(grad_key, ("dp", "seq"), scatter_dimension=0, tiled=True),
        lax.psum_scatter(grad_value, ("dp", "seq"), scatter_dimension=0, tiled=True),
        lax.psum_scatter(grad_value_b, ("dp", "seq"), scatter_dimension=0, tiled=True),
        lax.psum_scatter(grad_out, ("dp", "seq"), scatter_dimension=0, tiled=True),
        lax.psum_scatter(grad_out_b, ("dp", "seq"), scatter_dimension=0, tiled=True),
        lax.psum_scatter(grad_gain_two, ("dp", "seq"), scatter_dimension=0, tiled=True),
        lax.psum_scatter(grad_shift_two, ("dp", "seq"), scatter_dimension=0, tiled=True),
        lax.psum_scatter(grad_up, ("dp", "seq"), scatter_dimension=0, tiled=True),
        lax.psum_scatter(grad_up_b, ("dp", "seq"), scatter_dimension=0, tiled=True),
        lax.psum_scatter(grad_down, ("dp", "seq"), scatter_dimension=0, tiled=True),
        lax.psum_scatter(grad_down_b, ("dp", "seq"), scatter_dimension=0, tiled=True),
    )
    return (block_out, input_grad) + tuple(every_shard)


def solution(mesh):
    return jax.shard_map(
        per_device,
        mesh=mesh,
        in_specs=(
            P("dp", "seq", None),
            P("dp", "seq", None),
            P("dp"),
            P("dp", None),
            P(("dp", "seq")),
            P(("dp", "seq")),
            P(("dp", "seq"), None),
            P(("dp", "seq")),
            P(("dp", "seq"), None),
            P(("dp", "seq"), None),
            P(("dp", "seq")),
            P(("dp", "seq"), None),
            P(("dp", "seq")),
            P(("dp", "seq")),
            P(("dp", "seq")),
            P(("dp", "seq"), None),
            P(("dp", "seq")),
            P(("dp", "seq"), None),
            P(("dp", "seq")),
        ),
        out_specs=(
            P("dp", "seq", None),
            P("dp", "seq", None),
            P(("dp", "seq")),
            P(("dp", "seq")),
            P(("dp", "seq"), None),
            P(("dp", "seq")),
            P(("dp", "seq"), None),
            P(("dp", "seq"), None),
            P(("dp", "seq")),
            P(("dp", "seq"), None),
            P(("dp", "seq")),
            P(("dp", "seq")),
            P(("dp", "seq")),
            P(("dp", "seq"), None),
            P(("dp", "seq")),
            P(("dp", "seq"), None),
            P(("dp", "seq")),
        ),
        check_vma=False,
    )
```

profile of v0, /device:TPU:0, one launch (start us, length us, event | category | flops | bytes accessed | tf_op | source)
XLA Modules:
  0.0 1859.5 jit_solution(8726085616884812577)
XLA Ops:
  7.3 1.7 convert_element_type.187
  9.1 1.5 convert_element_type.185
  10.8 1.5 convert_element_type.181
  12.4 1.5 convert_element_type.191
  14.0 1.8 convert_element_type.199
  18.8 42.5 %all-reduce.18 = (bf16[1024]{0:T(1024)(128)(2,1)S(1)}, bf16[1024]{0:T(1024)(128)(2,1)S(1)}, bf16[1024]{0:T(1024)(128)(2,1)S(1)}, bf16[1024]{0:T(1024)(128)(2,1)S...) all-reduce(bf16[1024]{0:T(1024)(128)(2,1)S(1)} %dynamic-update-slic, ...), channel_id=1, replica_groups=mesh['dp'=8,'seq'=4] {'dp','seq'}, use_global_device_ids=true, to_apply=%add.1 | all-reduce | flops 8192 | bytes 32768
  63.5 7.6 all-gather.12.cloned.1.call-done
  71.1 3.2 fusion.21
  75.5 54.4 %all-gather.10.cloned.1.call-done = bf16[1024,1024]{1,0:T(8,128)(2,1)} async-done(((bf16[32,1024]{1,0:T(8,128)(2,1)}), bf16[1024,1024]{1,0:T(8,128)(2,1)}) %all-gather.10.cloned.1.call-update) | async-done | bytes 2097168 | tf_op jit(solution)/shard_map/all_gather | solution.py:140
  129.9 2.4 convolution_convert_fusion.1
  132.5 56.2 %all-gather.8.cloned.1.call-done = bf16[1024,1024]{1,0:T(8,128)(2,1)} async-done(((bf16[32,1024]{1,0:T(8,128)(2,1)}), bf16[1024,1024]{1,0:T(8,128)(2,1)}) %all-gather.8.cloned.1.call-update) | async-done | bytes 2097168 | tf_op jit(solution)/shard_map/all_gather | solution.py:138
  188.7 2.6 fusion.20
  193.5 5.7 copy.101
  199.3 3.9 all-to-all-start
  203.1 80.6 %all-to-all-done = bf16[2,145,3,1024]{1,0,2,3:T(2,128)(2,1)S(1)} async-done(((bf16[2,145,3,1024]{1,0,2,3:T(2,128)(2,1)}), bf16[2,145,3,1024]{1,0,2,3:T(2,128)(2,1)S(1)}, u32[]{:S(2)}, u32[]{:S(2)}) %all-to-all-start) | async-done | bytes 1781792 | tf_op jit(solution)/shard_map/all_to_all | solution.py:179
  283.8 4.1 copy.145
  287.8 5.4 reshape.335
  293.2 9.8 while.22
  293.5 1.4 fusion.98
  296.3 1.7 fusion.100
  298.4 1.4 fusion.98
  301.2 1.7 fusion.100
  304.2 3.5 all-to-all-start.1
  308.4 82.6 %all-gather = bf16[32,1,128]{2,1,0:T(2,128)(2,1)S(1)} all-gather(bf16[1,1,128]{2,1,0:T(2,128)(2,1)S(1)} %convert_bitcast_fusion), channel_id=1, replica_groups=mesh['dp'=8,'seq'=4] {'dp','seq'}, dimensions={0}, use_global_device_ids=true | all-gather | bytes 8448 | tf_op jit(solution)/shard_map/all_gather | solution.py:148
  392.6 3.0 fusion.36
  396.0 8.8 convolution_add_fusion
  404.8 42.8 %all-gather.18.cloned.1.call-done = bf16[4096,1024]{1,0:T(8,128)(2,1)} async-done(((bf16[128,1024]{1,0:T(8,128)(2,1)}), bf16[4096,1024]{1,0:T(8,128)(2,1)}) %all-gather.18.cloned.1.call-update) | async-done | bytes 8388624 | tf_op jit(solution)/shard_map/all_gather | solution.py:149
  447.7 8.7 fusion.19
  456.4 2.5 reshape.310
  458.8 3.7 fusion.32
  462.6 2.4 reshape.311
  465.0 9.0 convert_reduce_fusion
  474.0 6.4 multiply_reduce_fusion.1
  484.3 3.7 copy.109
  487.9 4.3 all-to-all-start.2
  492.3 4.4 fusion.29
  496.7 35.9 %all-to-all-done.2 = bf16[2,145,1024]{1,0,2:T(2,128)(2,1)} async-done(((bf16[2,145,1024]{1,0,2:T(2,128)(2,1)}), bf16[2,145,1024]{1,0,2:T(2,128)(2,1)}, u32[]{:S(2)}, u32[]{:S(2)}) %all-to-all-start.2) | async-done | bytes 593952 | tf_op jit(solution)/shard_map/all_to_all | solution.py:213
  532.6 3.0 copy.147
  535.6 2.7 reshape.334
  538.3 21.9 %while.23 = (s32[]{:T(128)}, bf16[2,580,3,256]{1,3,2,0:T(8,128)(2,1)}, bf16[2,580,3,256]{1,3,2,0:T(8,128)(2,1)S(1)}, s32[2,580]{1,0:T(2,128)S(1)}, f32[2,4,580]{...) while((s32[]{:T(128)}, bf16[2,580,3,256]{1,3,2,0:T(8,128)(2,1)}, ...), condition=%wide.region_12.13_spmd, body=%wide.region_10.12_spmd.sunk | while | flops 884781312 | bytes 63784960 | solution.py:214
  539.7 1.5 fusion.113
  541.2 2.0 multiply_reduce_fusion.10
  543.2 1.9 multiply_convert_fusion.6
  550.6 1.5 fusion.113
  552.1 2.0 multiply_reduce_fusion.10
  554.2 1.9 multiply_convert_fusion.6
  560.1 5.2 copy.114
  565.4 4.5 all-to-all-start.3
  571.3 61.0 %all-to-all-done.3 = bf16[2,580,3,256]{3,0,2,1:T(2,128)(2,1)} async-done(((bf16[2,580,3,256]{3,0,2,1:T(2,128)(2,1)}), bf16[2,580,3,256]{3,0,2,1:T(2,128)(2,1)}, u32[]{:S(2)}, u32[]{:S(2)}) %all-to-all-start.3) | async-done | bytes 1781792 | tf_op jit(solution)/shard_map/all_to_all | solution.py:215
  632.3 1.8 copy.146
  634.1 2.0 copy.116
  636.0 3.0 reshape.313
  639.0 3.3 fusion.23
  642.4 3.3 fusion.22
  645.7 3.4 fusion.25
  650.4 10.0 fusion.33
  661.8 11.0 fusion.26
  675.3 2.6 fusion.24
  683.5 39.7 %all-reduce.17 = (f32[1024]{0:T(1024)S(1)}, f32[1024]{0:T(1024)S(1)}, f32[1024]{0:T(1024)S(1)}, f32[1024]{0:T(1024)S(1)}, f32[1024]{0:T(1024)S(1)}, /*index=5*/f...) all-reduce(f32[1024]{0:T(1024)S(1)} %get-tuple-element.183, ...), channel_id=2, replica_groups=mesh['dp'=8,'seq'=4] {'dp','seq'}, use_global_device_ids=true, to_apply=%region_16.17.clone | all-reduce | flops 12288 | bytes 98304
  728.5 95.1 %reduce-scatter.7.cloned.1.call-done = f32[32,1024]{1,0:T(8,128)} async-done(((f32[1024,1024]{1,0:T(8,128)}), f32[32,1024]{1,0:T(8,128)}) %reduce-scatter.7.cloned.1.call-update) | async-done | bytes 131088 | tf_op jit(solution)/shard_map/reduce_scatter | solution.py:238
  823.6 151.1 %reduce-scatter.9.cloned.1.call-done = f32[32,1024]{1,0:T(8,128)} async-done(((f32[1024,1024]{1,0:T(8,128)}), f32[32,1024]{1,0:T(8,128)}) %reduce-scatter.9.cloned.1.call-update) | async-done | bytes 131088 | tf_op jit(solution)/shard_map/reduce_scatter | solution.py:240
  974.7 150.8 %reduce-scatter.11.cloned.1.call-done = f32[32,1024]{1,0:T(8,128)} async-done(((f32[1024,1024]{1,0:T(8,128)}), f32[32,1024]{1,0:T(8,128)}) %reduce-scatter.11.cloned.1.call-update) | async-done | bytes 131088 | tf_op jit(solution)/shard_map/reduce_scatter | solution.py:241
  1125.5 362.2 %reduce-scatter.15.cloned.1.call-done = f32[32,4096]{1,0:T(8,128)} async-done(((f32[1024,4096]{1,0:T(8,128)}), f32[32,4096]{1,0:T(8,128)}) %reduce-scatter.15.cloned.1.call-update) | async-done | bytes 524304 | tf_op jit(solution)/shard_map/reduce_scatter | solution.py:247
  1487.7 364.7 %reduce-scatter.17.cloned.1.call-done = f32[128,1024]{1,0:T(8,128)} async-done(((f32[4096,1024]{1,0:T(8,128)}), f32[128,1024]{1,0:T(8,128)}) %reduce-scatter.17.cloned.1.call-update) | async-done | bytes 524304 | tf_op jit(solution)/shard_map/reduce_scatter | solution.py:249
  (237 shorter events, 47.1 us)
Async XLA Ops:
  7.2 8.7 copy-start.22
  7.2 9.4 copy-start.35
  7.2 9.4 copy-start.36
  7.2 9.5 copy-start.37
  7.2 9.5 copy-start.38
  7.2 9.5 copy-start.39
  7.3 9.5 copy-start.40
  7.3 9.5 copy-start.41
  7.3 9.5 copy-start.42
  7.3 9.5 copy-start.7
  7.3 63.8 %all-gather.12.cloned.1.call-start = ((), (), s32[]{:S(2)}) async-start(), calls=%async_computation.12 | async-start | bytes 2162688 | tf_op jit(solution)/shard_map/all_gather | solution.py:141
  9.1 120.8 %all-gather.10.cloned.1.call-start = ((), (), s32[]{:S(2)}) async-start(), calls=%async_computation.11 | async-start | bytes 2162688 | tf_op jit(solution)/shard_map/all_gather | solution.py:140
  10.7 178.0 %all-gather.8.cloned.1.call-start = ((), (), s32[]{:S(2)}) async-start(), calls=%async_computation.10 | async-start | bytes 2162688 | tf_op jit(solution)/shard_map/all_gather | solution.py:138
  12.3 380.3 %all-gather.14.cloned.1.call-start = ((), (), s32[]{:S(2)}) async-start(), calls=%async_computation.13 | async-start | bytes 2162688 | tf_op jit(solution)/shard_map/all_gather | solution.py:143
  13.9 382.0 %all-gather.16.cloned.1.call-start = ((), (), s32[]{:S(2)}) async-start(), calls=%async_computation.14 | async-start | bytes 8650752 | tf_op jit(solution)/shard_map/all_gather | solution.py:147
  15.8 431.9 %all-gather.18.cloned.1.call-start = ((), (), s32[]{:S(2)}) async-start(), calls=%async_computation.15 | async-start | bytes 8650752 | tf_op jit(solution)/shard_map/all_gather | solution.py:149
  17.1 57.2 %copy-start.2 = (f32[290,1024]{1,0:T(8,128)}, f32[290,1024]{1,0:T(8,128)S(1)}, u32[]{:S(2)}) copy-start(f32[290,1024]{1,0:T(8,128)S(1)} %reshape.308) | copy-start | bytes 3563524
  61.3 9.8 copy-start.26
  61.3 9.8 copy-start.24
  61.9 9.2 copy-start.16
  62.9 11.4 copy-start.18
  63.1 11.2 copy-start.28
  63.2 11.1 copy-start.30
  63.5 66.4 %copy-start.21 = (bf16[290,1024]{1,0:T(8,128)(2,1)}, bf16[290,1024]{1,0:T(8,128)(2,1)S(1)}, u32[]{:S(2)}) copy-start(bf16[290,1024]{1,0:T(8,128)(2,1)S(1)} %add_convert_fusion.2) | copy-start | bytes 1781764
  199.3 84.5 %all-to-all-start = ((bf16[2,145,3,1024]{1,0,2,3:T(2,128)(2,1)}), bf16[2,145,3,1024]{1,0,2,3:T(2,128)(2,1)S(1)}, u32[]{:S(2)}, u32[]{:S(2)}) async-start(bf16[2,145,3,1024]{1,0,2,3:T(2,128)(2,1)} %copy.101), calls=%async_computation | async-start | bytes 6291456 | tf_op jit(solution)/shard_map/all_to_all | solution.py:179
  287.8 5.4 copy-start.20
  287.8 5.4 copy-start.23
  303.0 5.4 copy-start.43
  304.2 86.8 %all-to-all-start.1 = ((bf16[2,580,256]{2,0,1:T(2,128)(2,1)}), bf16[2,580,256]{2,0,1:T(2,128)(2,1)S(1)}, u32[]{:S(2)}, u32[]{:S(2)}) async-start(bf16[2,580,256]{2,0,1:T(2,128)(2,1)} %copy.105), calls=%async_computation.1 | async-start | bytes 1187840 | tf_op jit(solution)/shard_map/all_to_all | solution.py:181
  395.7 84.8 %copy-start = (f32[290,1024]{1,0:T(8,128)}, f32[290,1024]{1,0:T(8,128)S(1)}, u32[]{:S(2)}) copy-start(f32[290,1024]{1,0:T(8,128)S(1)} %get-tuple-element.246) | copy-start | bytes 3563524
  474.0 6.5 copy-start.12
  474.0 6.5 copy-start.9
  480.5 2.0 copy-start.34
  480.9 1.0 copy-start.4
  484.3 8.0 copy-start.5
  487.9 44.6 %all-to-all-start.2 = ((bf16[2,145,1024]{1,0,2:T(2,128)(2,1)}), bf16[2,145,1024]{1,0,2:T(2,128)(2,1)}, u32[]{:S(2)}, u32[]{:S(2)}) async-start(bf16[2,145,1024]{1,0,2:T(2,128)(2,1)} %copy.109), calls=%async_computation.2 | async-start | bytes 2097152 | tf_op jit(solution)/shard_map/all_to_all | solution.py:213
  492.2 236.2 %reduce-scatter.13.cloned.1.call-start = ((), (), s32[]{:S(2)}) async-start(), calls=%async_computation.19 | async-start | bytes 4325376 | tf_op jit(solution)/shard_map/reduce_scatter | solution.py:243
  546.2 1.6 copy-start.14
  547.9 1.3 copy-start.15
  557.1 1.6 copy-start.14
  558.8 1.3 copy-start.15
  565.3 4.6 copy-start.8
  565.3 4.6 copy-start.17
  565.3 4.6 copy-start.19
  565.3 4.6 copy-start.25
  565.3 4.6 copy-start.27
  565.4 66.9 %all-to-all-start.3 = ((bf16[2,580,3,256]{3,0,2,1:T(2,128)(2,1)}), bf16[2,580,3,256]{3,0,2,1:T(2,128)(2,1)}, u32[]{:S(2)}, u32[]{:S(2)}) async-start(bf16[2,580,3,256]{3,0,2,1:T(2,128)(2,1)} %copy.114), calls=%async_computation.3 | async-start | bytes 3563520 | tf_op jit(solution)/shard_map/all_to_all | solution.py:215
  569.9 253.7 %reduce-scatter.7.cloned.1.call-start = ((), (), s32[]{:S(2)}) async-start(), calls=%async_computation.16 | async-start | bytes 4325376 | tf_op jit(solution)/shard_map/reduce_scatter | solution.py:238
  642.4 332.4 %reduce-scatter.9.cloned.1.call-start = ((), (), s32[]{:S(2)}) async-start(), calls=%async_computation.17 | async-start | bytes 4325376 | tf_op jit(solution)/shard_map/reduce_scatter | solution.py:240
  645.7 479.8 %reduce-scatter.11.cloned.1.call-start = ((), (), s32[]{:S(2)}) async-start(), calls=%async_computation.18 | async-start | bytes 4325376 | tf_op jit(solution)/shard_map/reduce_scatter | solution.py:241
  649.1 1.3 copy-start.1
  649.2 838.6 %reduce-scatter.15.cloned.1.call-start = ((), (), s32[]{:S(2)}) async-start(), calls=%async_computation.20 | async-start | bytes 17301504 | tf_op jit(solution)/shard_map/reduce_scatter | solution.py:247
  660.5 1.3 copy-start.10
  660.5 1191.9 %reduce-scatter.17.cloned.1.call-start = ((), (), s32[]{:S(2)}) async-start(), calls=%async_computation.21 | async-start | bytes 17301504 | tf_op jit(solution)/shard_map/reduce_scatter | solution.py:249
  672.8 1.1 copy-start.11
  675.3 2.6 copy-start.13
  677.9 1.3 copy-start.3
  677.9 1.3 copy-start.29
  677.9 1.3 copy-start.31
  677.9 2.0 copy-start.33
  679.9 1.3 copy-start.6
  681.7 1.8 copy-start.32
Sparse Core Ops, SparseCore 0:
  11.6 59.4 all-gather.11
  74.6 55.2 all-gather.9
  133.4 55.1 all-gather.7
  192.0 93.6 all-gather.13
  289.1 79.6 all-gather.15
  372.1 75.5 all-gather.17
  496.8 176.0 reduce-scatter.12
  675.7 147.7 reduce-scatter.6
  826.4 148.2 reduce-scatter.8
  977.4 148.0 reduce-scatter.10
  1128.4 359.2 reduce-scatter.14
  1490.5 361.9 reduce-scatter.16
where the time goes:
time: 1870 us; the launch traced here: 1860 us
  waiting for transfers between devices  1460 us (78%)
  blocking collectives  165 us (9%)
  matrix products  104 us (6%)
  local copies, waits for them, and re-layouts  69.7 us (4%)
  other arithmetic  25.2 us (1%)
    reduce_scatter x1, waiting for transfers between devices, per_device(): lax.psum_scatter(grad_down, ('dp', 'seq'), scatter_dimension=0, tiled=True)  365 us
    reduce_scatter x1, waiting for transfers between devices, per_device(): lax.psum_scatter(grad_up, ('dp', 'seq'), scatter_dimension=0, tiled=True)  362 us
    reduce_scatter x1, waiting for transfers between devices, per_device(): lax.psum_scatter(grad_key, ('dp', 'seq'), scatter_dimension=0, tiled=True)  151 us
    reduce_scatter x1, waiting for transfers between devices, per_device(): lax.psum_scatter(grad_value, ('dp', 'seq'), scatter_dimension=0, tiled=True)  151 us
    reduce_scatter x1, waiting for transfers between devices, per_device(): lax.psum_scatter(grad_query, ('dp', 'seq'), scatter_dimension=0, tiled=True)  95.1 us
    all_gather x1, blocking collectives, per_device(): lax.all_gather(b_up.astype(jnp.bfloat16), ('dp', 'seq'), axis=0, tiled=True)  82.6 us
    unnamed x2, blocking collectives  82.2 us
    all_to_all x1, waiting for transfers between devices, per_device(): lax.all_to_all(stacked, 'seq', split_axis=3, concat_axis=1, tiled=True)  80.6 us
  transfers between devices with their start and end apart: 16, of which 12 were waited for; matrix products, arithmetic and copies ran while one was open for 8% of the time, Pallas kernels for 0%

commit v1 on v0

--- a/solution.py
+++ b/solution.py
@@ -1,12 +1,29 @@
+import functools
 import jax
 import jax.numpy as jnp
 from jax import lax
 from jax.sharding import PartitionSpec as P
+from jax.lax import all_to_all, axis_size
 
 HD = 64
 EPSILON = 1e-05
 SLOPE = 1.702
 MASKED = -1000000000.0
+
+
+def follow_the_squares(u_in, mesh_dim, along_dim, in_dim):
+    return jnp.concatenate(
+        all_to_all(
+            jnp.stack(jnp.split(u_in, axis_size(mesh_dim), axis=along_dim), axis=0),
+            axis_name=mesh_dim,
+            split_axis=0,
+            concat_axis=0,
+        ),
+        axis=in_dim,
+    )
+
+
+stocks_settle = functools.partial(follow_the_squares, mesh_dim="seq", along_dim=1, in_dim=3)
 
 
 def norm_stats(values):
@@ -212,9 +229,7 @@
     )
     grad_by_heads = lax.all_to_all(grad_mixed, "seq", split_axis=2, concat_axis=1, tiled=True)
     grad_stacked = lax.map(attend_back, (by_heads, grad_by_heads, log_total, key_mask))
-    grad_tok = lax.all_to_all(grad_stacked, "seq", split_axis=1, concat_axis=3, tiled=True).reshape(
-        row_count, 3, width
-    )
+    grad_tok = stocks_settle(grad_stacked).reshape(row_count, 3, width)
     grad_q_rows = grad_tok[:, 0]
     grad_k_rows = grad_tok[:, 1]
     grad_v_rows = grad_tok[:, 2]

time: 1870 us -> 1870 us (level)
  no operation moved by 1% of the time
where the time goes in v1:
time: 1870 us; the launch traced here: 1860 us
  waiting for transfers between devices  1460 us (78%)
  blocking collectives  164 us (9%)
  matrix products  104 us (6%)
  local copies, waits for them, and re-layouts  69.3 us (4%)
  other arithmetic  29.4 us (2%)
    reduce_scatter x1, waiting for transfers between devices, per_device(): lax.psum_scatter(grad_down, ('dp', 'seq'), scatter_dimension=0, tiled=True)  365 us
    reduce_scatter x1, waiting for transfers between devices, per_device(): lax.psum_scatter(grad_up, ('dp', 'seq'), scatter_dimension=0, tiled=True)  362 us
    reduce_scatter x1, waiting for transfers between devices, per_device(): lax.psum_scatter(grad_value, ('dp', 'seq'), scatter_dimension=0, tiled=True)  151 us
    reduce_scatter x1, waiting for transfers between devices, per_device(): lax.psum_scatter(grad_key, ('dp', 'seq'), scatter_dimension=0, tiled=True)  150 us
    reduce_scatter x1, waiting for transfers between devices, per_device(): lax.psum_scatter(grad_query, ('dp', 'seq'), scatter_dimension=0, tiled=True)  91.1 us
    all_gather x1, blocking collectives, per_device(): lax.all_gather(b_up.astype(jnp.bfloat16), ('dp', 'seq'), axis=0, tiled=True)  82.8 us
    unnamed x2, blocking collectives  81.4 us
    all_to_all x1, waiting for transfers between devices, per_device(): lax.all_to_all(stacked, 'seq', split_axis=3, concat_axis=1, tiled=True)  80.5 us
  transfers between devices with their start and end apart: 16, of which 12 were waited for; matrix products, arithmetic and copies ran while one was open for 8% of the time, Pallas kernels for 0%

profile of v1, /device:TPU:0, one launch (start us, length us, event | category | flops | bytes accessed | tf_op | source)
XLA Modules:
  0.0 1859.5 jit_solution(4375514169695994829)
XLA Ops:
  7.3 1.7 convert_element_type.187
  9.1 1.5 convert_element_type.185
  10.8 1.5 convert_element_type.181
  12.4 1.5 convert_element_type.191
  14.0 1.8 convert_element_type.199
  18.8 42.5 %all-reduce.18 = (bf16[1024]{0:T(1024)(128)(2,1)S(1)}, bf16[1024]{0:T(1024)(128)(2,1)S(1)}, bf16[1024]{0:T(1024)(128)(2,1)S(1)}, bf16[1024]{0:T(1024)(128)(2,1)S...) all-reduce(bf16[1024]{0:T(1024)(128)(2,1)S(1)} %dynamic-update-slic, ...), channel_id=1, replica_groups=mesh['dp'=8,'seq'=4] {'dp','seq'}, use_global_device_ids=true, to_apply=%add.1 | all-reduce | flops 8192 | bytes 32768
  63.5 7.6 all-gather.12.cloned.1.call-done
  71.1 3.2 fusion.21
  75.5 54.4 %all-gather.10.cloned.1.call-done = bf16[1024,1024]{1,0:T(8,128)(2,1)} async-done(((bf16[32,1024]{1,0:T(8,128)(2,1)}), bf16[1024,1024]{1,0:T(8,128)(2,1)}) %all-gather.10.cloned.1.call-update) | async-done | bytes 2097168 | tf_op jit(solution)/shard_map/all_gather | solution.py:157
  129.9 2.4 convolution_convert_fusion.1
  132.5 56.2 %all-gather.8.cloned.1.call-done = bf16[1024,1024]{1,0:T(8,128)(2,1)} async-done(((bf16[32,1024]{1,0:T(8,128)(2,1)}), bf16[1024,1024]{1,0:T(8,128)(2,1)}) %all-gather.8.cloned.1.call-update) | async-done | bytes 2097168 | tf_op jit(solution)/shard_map/all_gather | solution.py:155
  188.7 2.6 fusion.20
  193.5 5.8 copy.102
  199.3 3.9 all-to-all-start
  203.2 80.5 %all-to-all-done = bf16[2,145,3,1024]{1,0,2,3:T(2,128)(2,1)S(1)} async-done(((bf16[2,145,3,1024]{1,0,2,3:T(2,128)(2,1)}), bf16[2,145,3,1024]{1,0,2,3:T(2,128)(2,1)S(1)}, u32[]{:S(2)}, u32[]{:S(2)}) %all-to-all-start) | async-done | bytes 1781792 | tf_op jit(solution)/shard_map/all_to_all | solution.py:196
  283.7 4.1 copy.146
  287.8 5.4 reshape.334
  293.2 9.7 while.22
  296.3 1.7 fusion.100
  298.3 1.4 fusion.98
  301.1 1.7 fusion.100
  304.2 3.5 all-to-all-start.1
  308.4 82.8 %all-gather = bf16[32,1,128]{2,1,0:T(2,128)(2,1)S(1)} all-gather(bf16[1,1,128]{2,1,0:T(2,128)(2,1)S(1)} %convert_bitcast_fusion), channel_id=1, replica_groups=mesh['dp'=8,'seq'=4] {'dp','seq'}, dimensions={0}, use_global_device_ids=true | all-gather | bytes 8448 | tf_op jit(solution)/shard_map/all_gather | solution.py:165
  392.9 3.0 fusion.36
  396.2 8.8 convolution_add_fusion
  405.0 42.7 %all-gather.18.cloned.1.call-done = bf16[4096,1024]{1,0:T(8,128)(2,1)} async-done(((bf16[128,1024]{1,0:T(8,128)(2,1)}), bf16[4096,1024]{1,0:T(8,128)(2,1)}) %all-gather.18.cloned.1.call-update) | async-done | bytes 8388624 | tf_op jit(solution)/shard_map/all_gather | solution.py:166
  447.7 8.7 fusion.19
  456.4 2.5 reshape.309
  458.9 3.7 fusion.32
  462.6 2.4 reshape.310
  465.0 9.0 convert_reduce_fusion
  474.0 6.4 multiply_reduce_fusion.1
  484.3 3.7 copy.110
  488.0 4.3 all-to-all-start.2
  492.3 4.4 fusion.29
  496.7 35.9 %all-to-all-done.2 = bf16[2,145,1024]{1,0,2:T(2,128)(2,1)} async-done(((bf16[2,145,1024]{1,0,2:T(2,128)(2,1)}), bf16[2,145,1024]{1,0,2:T(2,128)(2,1)}, u32[]{:S(2)}, u32[]{:S(2)}) %all-to-all-start.2) | async-done | bytes 593952 | tf_op jit(solution)/shard_map/all_to_all | solution.py:230
  532.6 3.0 copy.147
  535.6 2.4 reshape.333
  538.1 21.9 %while.23 = (s32[]{:T(128)}, bf16[2,580,3,256]{1,3,2,0:T(8,128)(2,1)}, bf16[2,580,3,256]{1,3,2,0:T(8,128)(2,1)S(1)}, s32[2,580]{1,0:T(2,128)S(1)}, f32[2,4,580]{...) while((s32[]{:T(128)}, bf16[2,580,3,256]{1,3,2,0:T(8,128)(2,1)}, ...), condition=%wide.region_12.13_spmd, body=%wide.region_10.12_spmd.sunk | while | flops 884781312 | bytes 63784960 | solution.py:231
  539.5 1.5 fusion.113
  541.0 2.0 multiply_reduce_fusion.10
  543.1 1.9 multiply_convert_fusion.6
  550.4 1.5 fusion.113
  552.0 2.0 multiply_reduce_fusion.10
  554.0 1.9 multiply_convert_fusion.6
  559.9 4.5 copy.115
  565.7 4.2 pad_maximum_fusion.1
  569.9 4.5 all-to-all-start.3
  576.0 62.2 %all-to-all-done.3 = bf16[4,2,145,3,256]{4,1,3,2,0:T(2,128)(2,1)} async-done(((bf16[4,2,145,3,256]{4,1,3,2,0:T(2,128)(2,1)}), bf16[4,2,145,3,256]{4,1,3,2,0:T(2,128)(2,1)}, u32[]{:S(2)}, u32[]{:S(2)}) %all-to-all-start.3) | async-done | bytes 1781792 | tf_op jit(solution)/shard_map/all_to_all | solution.py:16
  638.3 3.4 copy.119
  641.7 2.9 reshape_reshape.3
  644.5 3.3 fusion.23
  647.9 3.3 fusion.22
  651.3 3.4 fusion.25
  656.0 10.0 fusion.33
  667.3 10.7 fusion.26
  680.5 2.6 fusion.24
  687.0 1.4 copy.123
  688.7 38.9 %all-reduce.17 = (f32[1024]{0:T(1024)S(1)}, f32[1024]{0:T(1024)S(1)}, f32[1024]{0:T(1024)S(1)}, f32[1024]{0:T(1024)S(1)}, f32[1024]{0:T(1024)S(1)}, /*index=5*/f...) all-reduce(f32[1024]{0:T(1024)S(1)} %get-tuple-element.183, ...), channel_id=2, replica_groups=mesh['dp'=8,'seq'=4] {'dp','seq'}, use_global_device_ids=true, to_apply=%region_16.17.clone | all-reduce | flops 12288 | bytes 98304
  732.9 91.1 %reduce-scatter.7.cloned.1.call-done = f32[32,1024]{1,0:T(8,128)} async-done(((f32[1024,1024]{1,0:T(8,128)}), f32[32,1024]{1,0:T(8,128)}) %reduce-scatter.7.cloned.1.call-update) | async-done | bytes 131088 | tf_op jit(solution)/shard_map/reduce_scatter | solution.py:253
  823.9 150.4 %reduce-scatter.9.cloned.1.call-done = f32[32,1024]{1,0:T(8,128)} async-done(((f32[1024,1024]{1,0:T(8,128)}), f32[32,1024]{1,0:T(8,128)}) %reduce-scatter.9.cloned.1.call-update) | async-done | bytes 131088 | tf_op jit(solution)/shard_map/reduce_scatter | solution.py:255
  974.4 150.8 %reduce-scatter.11.cloned.1.call-done = f32[32,1024]{1,0:T(8,128)} async-done(((f32[1024,1024]{1,0:T(8,128)}), f32[32,1024]{1,0:T(8,128)}) %reduce-scatter.11.cloned.1.call-update) | async-done | bytes 131088 | tf_op jit(solution)/shard_map/reduce_scatter | solution.py:256
  1125.2 362.3 %reduce-scatter.15.cloned.1.call-done = f32[32,4096]{1,0:T(8,128)} async-done(((f32[1024,4096]{1,0:T(8,128)}), f32[32,4096]{1,0:T(8,128)}) %reduce-scatter.15.cloned.1.call-update) | async-done | bytes 524304 | tf_op jit(solution)/shard_map/reduce_scatter | solution.py:262
  1487.5 364.7 %reduce-scatter.17.cloned.1.call-done = f32[128,1024]{1,0:T(8,128)} async-done(((f32[4096,1024]{1,0:T(8,128)}), f32[128,1024]{1,0:T(8,128)}) %reduce-scatter.17.cloned.1.call-update) | async-done | bytes 524304 | tf_op jit(solution)/shard_map/reduce_scatter | solution.py:264
  (238 shorter events, 48.5 us)
Async XLA Ops:
  7.2 8.7 copy-start.22
  7.2 9.4 copy-start.35
  7.2 9.4 copy-start.36
  7.2 9.5 copy-start.37
  7.2 9.5 copy-start.38
  7.2 9.5 copy-start.39
  7.3 9.5 copy-start.40
  7.3 9.5 copy-start.41
  7.3 9.5 copy-start.42
  7.3 9.5 copy-start.7
  7.3 63.8 %all-gather.12.cloned.1.call-start = ((), (), s32[]{:S(2)}) async-start(), calls=%async_computation.12 | async-start | bytes 2162688 | tf_op jit(solution)/shard_map/all_gather | solution.py:158
  9.1 120.8 %all-gather.10.cloned.1.call-start = ((), (), s32[]{:S(2)}) async-start(), calls=%async_computation.11 | async-start | bytes 2162688 | tf_op jit(solution)/shard_map/all_gather | solution.py:157
  10.7 178.0 %all-gather.8.cloned.1.call-start = ((), (), s32[]{:S(2)}) async-start(), calls=%async_computation.10 | async-start | bytes 2162688 | tf_op jit(solution)/shard_map/all_gather | solution.py:155
  12.3 380.5 %all-gather.14.cloned.1.call-start = ((), (), s32[]{:S(2)}) async-start(), calls=%async_computation.13 | async-start | bytes 2162688 | tf_op jit(solution)/shard_map/all_gather | solution.py:160
  13.9 382.2 %all-gather.16.cloned.1.call-start = ((), (), s32[]{:S(2)}) async-start(), calls=%async_computation.14 | async-start | bytes 8650752 | tf_op jit(solution)/shard_map/all_gather | solution.py:164
  15.8 431.9 %all-gather.18.cloned.1.call-start = ((), (), s32[]{:S(2)}) async-start(), calls=%async_computation.15 | async-start | bytes 8650752 | tf_op jit(solution)/shard_map/all_gather | solution.py:166
  17.1 57.2 %copy-start.2 = (f32[290,1024]{1,0:T(8,128)}, f32[290,1024]{1,0:T(8,128)S(1)}, u32[]{:S(2)}) copy-start(f32[290,1024]{1,0:T(8,128)S(1)} %reshape.307) | copy-start | bytes 3563524
  61.3 9.8 copy-start.26
  61.3 9.8 copy-start.24
  61.9 9.2 copy-start.16
  62.9 11.4 copy-start.18
  63.1 11.2 copy-start.28
  63.2 11.1 copy-start.30
  63.5 66.4 %copy-start.21 = (bf16[290,1024]{1,0:T(8,128)(2,1)}, bf16[290,1024]{1,0:T(8,128)(2,1)S(1)}, u32[]{:S(2)}) copy-start(bf16[290,1024]{1,0:T(8,128)(2,1)S(1)} %add_convert_fusion.2) | copy-start | bytes 1781764
  199.3 84.4 %all-to-all-start = ((bf16[2,145,3,1024]{1,0,2,3:T(2,128)(2,1)}), bf16[2,145,3,1024]{1,0,2,3:T(2,128)(2,1)S(1)}, u32[]{:S(2)}, u32[]{:S(2)}) async-start(bf16[2,145,3,1024]{1,0,2,3:T(2,128)(2,1)} %copy.102), calls=%async_computation | async-start | bytes 6291456 | tf_op jit(solution)/shard_map/all_to_all | solution.py:196
  287.8 5.4 copy-start.20
  287.8 5.4 copy-start.23
  303.0 5.4 copy-start.43
  304.2 87.1 %all-to-all-start.1 = ((bf16[2,580,256]{2,0,1:T(2,128)(2,1)}), bf16[2,580,256]{2,0,1:T(2,128)(2,1)S(1)}, u32[]{:S(2)}, u32[]{:S(2)}) async-start(bf16[2,580,256]{2,0,1:T(2,128)(2,1)} %copy.106), calls=%async_computation.1 | async-start | bytes 1187840 | tf_op jit(solution)/shard_map/all_to_all | solution.py:198
  395.9 84.6 %copy-start = (f32[290,1024]{1,0:T(8,128)}, f32[290,1024]{1,0:T(8,128)S(1)}, u32[]{:S(2)}) copy-start(f32[290,1024]{1,0:T(8,128)S(1)} %get-tuple-element.250) | copy-start | bytes 3563524
  474.0 6.5 copy-start.12
  474.0 6.5 copy-start.9
  480.5 2.0 copy-start.34
  481.0 1.0 copy-start.4
  484.3 8.0 copy-start.5
  488.0 44.6 %all-to-all-start.2 = ((bf16[2,145,1024]{1,0,2:T(2,128)(2,1)}), bf16[2,145,1024]{1,0,2:T(2,128)(2,1)}, u32[]{:S(2)}, u32[]{:S(2)}) async-start(bf16[2,145,1024]{1,0,2:T(2,128)(2,1)} %copy.110), calls=%async_computation.2 | async-start | bytes 2097152 | tf_op jit(solution)/shard_map/all_to_all | solution.py:230
  492.3 240.6 %reduce-scatter.13.cloned.1.call-start = ((), (), s32[]{:S(2)}) async-start(), calls=%async_computation.19 | async-start | bytes 4325376 | tf_op jit(solution)/shard_map/reduce_scatter | solution.py:258
  546.0 1.6 copy-start.14
  547.7 1.3 copy-start.15
  556.9 1.6 copy-start.14
  558.6 1.3 copy-start.15
  569.9 4.8 copy-start.8
  569.9 4.8 copy-start.17
  569.9 4.8 copy-start.19
  569.9 4.8 copy-start.25
  569.9 4.9 copy-start.27
  569.9 68.4 %all-to-all-start.3 = ((bf16[4,2,145,3,256]{4,1,3,2,0:T(2,128)(2,1)}), bf16[4,2,145,3,256]{4,1,3,2,0:T(2,128)(2,1)}, u32[]{:S(2)}, u32[]{:S(2)}) async-start(bf16[4,2,145,3,256]{4,1,3,2,0:T(2,128)(2,1)} %pad_maximum_fusion.1), calls=%async_computation.3 | async-start | bytes 3563520 | tf_op jit(solution)/shard_map/all_to_all | solution.py:16
  574.5 249.4 %reduce-scatter.7.cloned.1.call-start = ((), (), s32[]{:S(2)}) async-start(), calls=%async_computation.16 | async-start | bytes 4325376 | tf_op jit(solution)/shard_map/reduce_scatter | solution.py:253
  647.9 326.5 %reduce-scatter.9.cloned.1.call-start = ((), (), s32[]{:S(2)}) async-start(), calls=%async_computation.17 | async-start | bytes 4325376 | tf_op jit(solution)/shard_map/reduce_scatter | solution.py:255
  651.2 474.0 %reduce-scatter.11.cloned.1.call-start = ((), (), s32[]{:S(2)}) async-start(), calls=%async_computation.18 | async-start | bytes 4325376 | tf_op jit(solution)/shard_map/reduce_scatter | solution.py:256
  654.7 1.3 copy-start.1
  654.7 832.8 %reduce-scatter.15.cloned.1.call-start = ((), (), s32[]{:S(2)}) async-start(), calls=%async_computation.20 | async-start | bytes 17301504 | tf_op jit(solution)/shard_map/reduce_scatter | solution.py:262
  666.0 1.3 copy-start.10
  666.0 1186.2 %reduce-scatter.17.cloned.1.call-start = ((), (), s32[]{:S(2)}) async-start(), calls=%async_computation.21 | async-start | bytes 17301504 | tf_op jit(solution)/shard_map/reduce_scatter | solution.py:264
  678.0 1.1 copy-start.11
  680.5 2.6 copy-start.13
  683.1 1.3 copy-start.3
  683.1 1.3 copy-start.29
  683.2 1.3 copy-start.31
  683.2 2.0 copy-start.33
  685.1 1.3 copy-start.6
  686.9 1.8 copy-start.32
Sparse Core Ops, SparseCore 0:
  11.6 59.4 all-gather.11
  74.6 55.2 all-gather.9
  133.4 55.1 all-gather.7
  192.0 93.7 all-gather.13
  289.2 79.5 all-gather.15
  372.1 75.5 all-gather.17
  496.8 175.8 reduce-scatter.12
  675.6 148.2 reduce-scatter.6
  826.8 147.5 reduce-scatter.8
  977.1 148.0 reduce-scatter.10
  1128.1 359.4 reduce-scatter.14
  1490.2 361.9 reduce-scatter.16
